TPU v7x, 256 devices: a whole 4x4x8 slice. The times are simulated.
256 devices in a mesh: row: 8 (over x, y_hi), col: 32 (over z, y_lo, core).
Axes of the slice: x: 4, y: 4 (y_hi: 2, y_lo: 2; y = y_hi * 2 + y_lo), z: 8, core: 2. Of those that a mesh axis runs over, the one named last changes fastest.
Arguments:
- design: bfloat16 [2048, 24576], P('row', 'col'), may hold values from -6 to 6
- observations: bfloat16 [2048], P('row'), may hold values from -6 to 6
- filter_taps: float32 [64], replicated, may hold values from -0.5 to 0.5
- tap_count: int32 [4], replicated, may hold values from 32 to 64
- arc_id: int32 [2048], replicated, may hold values from 0 to 3, never falling along the last dimension, each value on 1 to 1024 neighbouring positions
Outputs:
- normal: float32 [24576, 24576], P('row', 'col')
- right_side: float32 [24576], P('col')
Inputs may be any that keep to these rules, and one draw needn't show every extreme that they name: `arc_id`: arc numbers never fall along the epochs; every arc holds 1 to 1024 epochs and one holds exactly 1024.
All inputs are finite; a program needn't handle non-finite values.
Results may differ from a plain program's by a relative error of at most 0.0031.
Values may be sent and summed in bfloat16 or wider, within the bound.
A program may use at most 128 MiB of HBM per device.

v0:
```python
import math

import jax
import jax.numpy as jnp
from jax import lax
from jax.sharding import Mesh
from jax.sharding import PartitionSpec as P

ROW = ("row_0", "row_1")


def from_behind(value, axis, steps):
    count = lax.axis_size(axis)
    leading, last = (max(0, -steps), min(count, count - steps))
    return lax.ppermute(value, axis, [(source, source + steps) for source in range(leading, last)])


def whole_of(x, axes, dim):
    for axis in reversed(axes):
        x = lax.all_gather(x, axis, axis=dim, tiled=True)
    return x


def on_device(design, observations, filter_taps, tap_count, arc_id):
    rows_here = design.shape[0]
    width = filter_taps.shape[0]
    arc_total = tap_count.shape[0]
    row_index = lax.axis_index(ROW)
    lower_design, lower_obs = from_behind(
        (design[rows_here - width :], observations[rows_here - width :]), ROW, 1
    )
    ext_design = jnp.concatenate([lower_design, design], axis=0)
    ext_obs = jnp.concatenate([lower_obs, observations], axis=0)
    first_epoch = row_index * rows_here
    target_epoch = first_epoch + jnp.arange(rows_here, dtype=jnp.int32)
    source_epoch = first_epoch - width + jnp.arange(rows_here + width, dtype=jnp.int32)
    lag_matrix = target_epoch[:, None] - source_epoch[None, :]
    arc_padded = jnp.concatenate([jnp.full((width,), -1, jnp.int32), arc_id])
    arc_target = lax.dynamic_slice_in_dim(arc_padded, first_epoch + width, rows_here)
    arc_source = lax.dynamic_slice_in_dim(arc_padded, first_epoch, rows_here + width)
    same_arc = (arc_target[:, None] == arc_source[None, :]) & (source_epoch[None, :] >= 0)
    arc_range = jnp.arange(arc_total, dtype=jnp.int32)
    target_taps = jnp.sum(
        jnp.where(arc_target[:, None] == arc_range[None, :], tap_count[None, :], 0), axis=1
    )
    tap_range = jnp.arange(width, dtype=jnp.int32)
    filter_rows = jnp.sum(
        jnp.where(
            lag_matrix[:, :, None] == tap_range[None, None, :], filter_taps, jnp.float32(0.0)
        ),
        axis=2,
    )
    filter_rows = jnp.where(
        same_arc & (lag_matrix < target_taps[:, None]), filter_rows, jnp.float32(0.0)
    )
    whitened = jnp.dot(
        filter_rows, ext_design.astype(jnp.float32), precision=lax.Precision.HIGHEST
    ).astype(jnp.bfloat16)
    white_obs = jnp.dot(
        filter_rows, ext_obs.astype(jnp.float32), precision=lax.Precision.HIGHEST
    ).astype(jnp.bfloat16)
    full_cols, full_obs = (whole_of(whitened, ROW, 0), whole_of(white_obs, ROW, 0))
    epochs = full_cols.shape[0]
    right_side = jnp.dot(full_obs, full_cols, preferred_element_type=jnp.float32) / math.sqrt(
        epochs
    )
    contract_dims = (((0,), (0,)), ((), ()))
    wide_panel = lax.all_gather(whitened, "col", axis=1, tiled=True)
    owner_panel = lax.all_to_all(wide_panel, ROW, split_axis=1, concat_axis=0, tiled=True)
    normal = lax.dot_general(
        owner_panel, full_cols, contract_dims, preferred_element_type=jnp.float32
    )
    return (normal / epochs, right_side)


def solution(mesh):
    finer = Mesh(mesh.devices.reshape(4, 2, mesh.shape["col"]), ("row_0", "row_1", "col"))
    in_specs = (P(ROW, "col"), P(ROW), P(), P(), P())
    out_specs = (P(ROW, "col"), P("col"))
    return jax.shard_map(
        on_device, mesh=finer, in_specs=in_specs, out_specs=out_specs, check_vma=False
    )
```

profile of v0, /device:TPU:1, one launch (start us, length us, event | category | flops | bytes accessed | tf_op | source)
XLA Modules:
  0.0 352.4 jit_solution(8104212342033234198)
XLA Ops:
  8.0 0.0 all-gather.5.cloned.1.call-start
  8.0 0.9 slice.6
  8.9 5.6 %collective-permute-start = (bf16[64,768]{1,0:T(8,128)(2,1)S(1)}, bf16[64,768]{1,0:T(8,128)(2,1)S(1)}, u32[]{:S(2)}, u32[]{:S(2)}) collective-permute-start(bf16[64,768]{1,0:T(8,128)(2,1)S(1)} %slice.6), channel_id=1, source_target_pairs={{0,32},{32,64},{64,96},{96,128},{128,160},{160,192},{192,224},{1,3... | collective-permute-start | bytes 294920 | tf_op jit(solution)/shard_map/ppermute | solution.py:15
  14.6 0.8 pad_dynamic-slice_fusion.1
  15.4 0.7 select_reduce_fusion.1
  16.1 0.8 pad_dynamic-slice_fusion
  16.9 0.1 broadcast_subtract_fusion
  17.0 8.0 %select_reduce_fusion = f32[256,320]{0,1:T(8,128)S(1)} fusion(f32[64]{0:T(128)} %param.7, s32[256,320]{0,1:T(8,128)S(1)} %broadcast_subtract_fusion), kind=kLoop, calls=%fused_computation | loop fusion | flops 15646720 | bytes 655616 | tf_op jit(solution)/shard_map/reduce_sum | solution.py:47
  25.1 0.0 collective-permute-done
  25.1 2.8 convolution_convert_fusion
  27.8 0.0 all-gather.5.cloned.1.call-update
  27.8 82.3 %all-gather.5.cloned.1.call-done = bf16[256,24576]{1,0:T(8,128)(2,1)} async-done(((bf16[256,768]{1,0:T(8,128)(2,1)}), bf16[256,24576]{1,0:T(8,128)(2,1)}) %all-gather.5.cloned.1.call-update) | async-done | bytes 12582928 | tf_op jit(solution)/shard_map/all_gather | solution.py:68
  110.2 10.9 %copy.12 = bf16[32,8,8,3072]{3,2,0,1:T(8,128)(2,1)} copy(bf16[32,8,8,3072]{3,2,1,0:T(8,128)(2,1)} %bitcast.16) | data formatting | bytes 25165824 | tf_op jit(solution)/shard_map/all_to_all | solution.py:69
  121.0 0.0 copy-start
  121.0 0.0 copy-start.1
  121.0 6.6 %all-to-all-start = ((bf16[256,8,3072]{2,0,1:T(8,128)(2,1)}), bf16[256,8,3072]{2,0,1:T(8,128)(2,1)}, u32[]{:S(2)}, u32[]{:S(2)}) async-start(bf16[256,8,3072]{2,0,1:T(8,128)(2,1)} %bitcast.15), calls=%async_computation | async-start | bytes 25165824 | tf_op jit(solution)/shard_map/all_to_all | solution.py:69
  127.6 0.0 all-gather.7.cloned.1.call-start
  127.6 0.0 copy-done
  127.7 146.7 %all_gather.16 = bf16[512,768]{1,0:T(8,128)(2,1)} all-gather(bf16[256,768]{1,0:T(8,128)(2,1)S(1)} %copy-done), channel_id=1, replica_groups=mesh['row_0'=4,'row_1'=2,'col'=32] {'row_1'}, dimensions={0}, use_global_device_ids=true | all-gather | bytes 1179648 | tf_op jit(solution)/shard_map/all_gather | solution.py:20
  274.4 0.0 all-gather.7.cloned.1.call-update
  274.4 0.0 copy-done.1
  274.4 0.1 slice.7
  274.5 2.2 collective-permute-start.1
  276.7 0.7 collective-permute-done.1
  277.4 0.1 pad_maximum_fusion
  277.5 0.4 fusion.3
  277.9 27.3 %all-gather = bf16[2,1,256]{2,1,0:T(2,128)(2,1)S(1)} all-gather(bf16[1,1,256]{2,1,0:T(2,128)(2,1)S(1)} %reshape.50), channel_id=1, replica_groups=mesh['row_0'=4,'row_1'=2,'col'=32] {'row_1'}, dimensions={0}, use_global_device_ids=true | all-gather | bytes 1536 | tf_op jit(solution)/shard_map/all_gather | solution.py:20
  305.2 16.2 %all-gather.1 = bf16[4,1,512]{2,1,0:T(2,128)(2,1)S(1)} all-gather(bf16[1,1,512]{2,1,0:T(2,128)(2,1)S(1)} %bitcast.18), channel_id=1, replica_groups=mesh['row_0'=4,'row_1'=2,'col'=32] {'row_0'}, dimensions={0}, use_global_device_ids=true | all-gather | bytes 5120 | tf_op jit(solution)/shard_map/all_gather | solution.py:20
  321.5 4.3 %all-gather.7.cloned.1.call-done = bf16[2048,768]{1,0:T(8,128)(2,1)} async-done(((bf16[512,768]{1,0:T(8,128)(2,1)}), bf16[2048,768]{1,0:T(8,128)(2,1)}) %all-gather.7.cloned.1.call-update) | async-done | bytes 3145744 | tf_op jit(solution)/shard_map/all_gather | solution.py:20
  325.7 2.4 convolution_reduce_fusion
  328.2 0.6 broadcast_multiply_fusion
  328.8 0.0 all-to-all-done
  328.8 16.2 %convolution_multiply_fusion = f32[3072,768]{1,0:T(8,128)} fusion(bf16[2048,3072]{1,0:T(8,128)(2,1)} %bitcast.1, bf16[2048,768]{1,0:T(8,128)(2,1)} %all-gather.7.cloned.1.call-done), kind=kOutput, calls=%fused_computation.3 | convolution fusion | flops 9666035712 | bytes 25165824 | tf_op jit(solution)/shard_map/dot_general | solution.py:70
  (4 shorter events, 0.0 us)
Async XLA Ops:
  8.0 102.2 %all-gather.5.cloned.1.call-start = ((), (), s32[]{:S(2)}) async-start(), calls=%async_computation.1 | async-start | bytes 12976128 | tf_op jit(solution)/shard_map/all_gather | solution.py:68
  8.9 16.1 %collective-permute-start = (bf16[64,768]{1,0:T(8,128)(2,1)S(1)}, bf16[64,768]{1,0:T(8,128)(2,1)S(1)}, u32[]{:S(2)}, u32[]{:S(2)}) collective-permute-start(bf16[64,768]{1,0:T(8,128)(2,1)S(1)} %slice.6), channel_id=1, source_target_pairs={{0,32},{32,64},{64,96},{96,128},{128,160},{160,192},{192,224},{1,3... | collective-permute-start | bytes 294920 | tf_op jit(solution)/shard_map/ppermute | solution.py:15
  121.0 6.6 %copy-start = (bf16[256,768]{1,0:T(8,128)(2,1)S(1)}, bf16[256,768]{1,0:T(8,128)(2,1)}, u32[]{:S(2)}) copy-start(bf16[256,768]{1,0:T(8,128)(2,1)} %convolution_convert_fusion) | copy-start | bytes 1179652
  121.0 153.4 %copy-start.1 = (bf16[256]{0:T(256)(128)(2,1)S(1)}, bf16[256]{0:T(256)(128)(2,1)}, u32[]{:S(2)}) copy-start(bf16[256]{0:T(256)(128)(2,1)} %param.6) | copy-start | bytes 1540
  121.0 207.7 %all-to-all-start = ((bf16[256,8,3072]{2,0,1:T(8,128)(2,1)}), bf16[256,8,3072]{2,0,1:T(8,128)(2,1)}, u32[]{:S(2)}, u32[]{:S(2)}) async-start(bf16[256,8,3072]{2,0,1:T(8,128)(2,1)} %bitcast.15), calls=%async_computation | async-start | bytes 25165824 | tf_op jit(solution)/shard_map/all_to_all | solution.py:69
  127.6 198.1 %all-gather.7.cloned.1.call-start = ((), (), s32[]{:S(2)}) async-start(), calls=%async_computation.2 | async-start | bytes 3932160 | tf_op jit(solution)/shard_map/all_gather | solution.py:20
  274.5 2.9 collective-permute-start.1
Sparse Core Ops, SparseCore 0:
  28.0 82.1 all-gather.4
Sparse Core Ops, SparseCore 1:
  274.5 51.2 all-gather.6
where the time goes:
time: 354 us; the launch traced here: 352 us
  blocking collectives  190 us (54%)
  waiting for transfers between devices  87.4 us (25%)
  matrix products  21.8 us (6%)
  between operations  15.6 us (4%)
  starting transfers between devices  14.5 us (4%)
  local copies, waits for them, and re-layouts  11.9 us (3%)
  other arithmetic  11.1 us (3%)
    all_gather x3, blocking collectives, whole_of(): x = lax.all_gather(x, axis, axis=dim, tiled=True)  190 us
    all_gather x1, waiting for transfers between devices, on_device(): wide_panel = lax.all_gather(whitened, 'col', axis=1, tiled=True)  82.3 us
    dot_general x1, matrix products, on_device(): lax.dot_general(owner_panel, full_cols, contract_dims, preferred_element_...  16.2 us
    all_to_all x1, local copies, waits for them, and re-layouts, on_device(): lax.all_to_all(wide_panel, ROW, split_axis=1, concat_axis=0, tiled=True)  10.9 us
    reduce_sum x1, other arithmetic, on_device(): jnp.sum(jnp.where(lag_matrix[:, :, None] == tap_range[None, None, :], fil...  8.03 us
    ppermute x2, starting transfers between devices, from_behind(): lax.ppermute(value, axis, [(source, source + steps) for source in range(l...  7.86 us
  transfers between devices with their start and end apart: 5, of which 3 were waited for; matrix products, arithmetic and copies ran while one was open for 4% of the time, Pallas kernels for 0%

commit v1 on v0

v1 whole, which is shorter than its diff:
```python
import functools
import math

import jax
import jax.numpy as jnp
from jax import lax
from jax.experimental import pallas as pl
from jax.experimental.pallas import tpu as pltpu
from jax.sharding import Mesh
from jax.sharding import PartitionSpec as P

MESH = pl.DeviceIdType.MESH
AXES = ("x", "yh", "z", "yl", "core")
NX, NZ = 4, 8
ROWS = 8
EXTRA = 16
UP, DOWN = 0, 1


def body(
    design_ref, obs_ref, taps_ref, count_ref, arc_ref,
    out_ref, right_ref,
    cols, panel, parts, halo, halo_obs, obs_own, taps_pad,
    halo_send, halo_recv, part_send, part_recv, own_sem, panel_send, panel_recv,
    col_send, col_recv, z_send, z_recv, lo_send, lo_recv, pair_send, pair_recv,
):
    x, yh, z = lax.axis_index("x"), lax.axis_index("yh"), lax.axis_index("z")
    yl, core = lax.axis_index("yl"), lax.axis_index("core")
    row = x * 2 + yh
    mine = yl * 2 + core
    here, width = design_ref.shape
    taps = taps_ref.shape[1]
    part = width // NZ
    deep = here * ROWS
    half = deep // 2
    quarter = deep // 4

    def at_row(r):
        return {"x": r // 2, "yh": lax.rem(r, 2)}

    barrier = pltpu.get_barrier_semaphore()
    peers = [at_row(lax.rem(row + i, ROWS)) for i in range(1, ROWS)]
    peers += [{"z": lax.rem(z + i, NZ)} for i in range(1, NZ)]
    peers += [{"yl": 1 - yl}, {"core": 1 - core}]
    for peer in peers:
        pl.semaphore_signal(barrier, inc=1, device_id=peer, device_id_type=MESH)

    obs_own[...] = jnp.broadcast_to(obs_ref[...].astype(jnp.float32), obs_own.shape).astype(jnp.bfloat16)
    halo[0:taps, :] = jnp.zeros((taps, width), jnp.bfloat16)
    pl.semaphore_wait(barrier, len(peers))

    started = []

    def send(src, dst, send_sem, recv_sem, device):
        copy = pltpu.make_async_remote_copy(
            src_ref=src, dst_ref=dst, send_sem=send_sem, recv_sem=recv_sem,
            device_id=device, device_id_type=MESH,
        )
        copy.start()
        started.append(copy)

    def arrived(dst, sem):
        pltpu.make_async_copy(dst, dst, sem).wait()

    after = at_row(lax.rem(row + 1, ROWS))
    send(design_ref.at[here - taps : here, :], halo.at[taps : 2 * taps, :], halo_send.at[0], halo_recv.at[0], after)
    send(obs_own, halo_obs, halo_send.at[1], halo_recv.at[1], after)

    taps_pad[...] = jnp.zeros(taps_pad.shape, jnp.float32)
    taps_pad[0:1, 0:taps] = taps_ref[...]
    line = jnp.broadcast_to(taps_pad[0:1, :], (here, here))
    toeplitz = pltpu.roll(line, 0, 1, stride=1, stride_axis=0).T
    target = lax.broadcasted_iota(jnp.int32, (here, here), 0)
    source = lax.broadcasted_iota(jnp.int32, (here, here), 1)
    lag = target - source
    own = lag >= 0
    lag = jnp.where(own, lag, lag + here)
    arc_here = jnp.broadcast_to(arc_ref[pl.ds(row, 1), :], (here, here))
    arc_before = jnp.broadcast_to(arc_ref[pl.ds(jnp.maximum(row - 1, 0), 1), :], (here, here))
    arc_before = jnp.where(row > 0, arc_before, -1)
    arc_target = arc_here.T
    arc_source = jnp.where(own, arc_here, arc_before)
    limit = jnp.zeros((here, here), jnp.int32)
    for a in range(count_ref.shape[0]):
        limit = jnp.where(arc_target == a, count_ref[a], limit)
    rows_f = jnp.where((arc_target == arc_source) & (lag < limit) & (lag < taps), toeplitz, 0.0)

    def three(value):
        high = value.astype(jnp.bfloat16)
        rest = value - high.astype(jnp.float32)
        middle = rest.astype(jnp.bfloat16)
        return high, middle, (rest - middle.astype(jnp.float32)).astype(jnp.bfloat16)

    own_terms = three(jnp.where(own, rows_f, 0.0))
    halo_terms = three(jnp.where(own, 0.0, rows_f)[0 : 2 * taps, here - 2 * taps :])
    by_lane = (((1,), (1,)), ((), ()))

    def total(terms, value):
        return sum(jnp.dot(t, value, preferred_element_type=jnp.float32) for t in terms[::-1])

    def total_lanes(terms, value):
        return sum(
            lax.dot_general(value, t, by_lane, preferred_element_type=jnp.float32) for t in terms[::-1]
        )

    white = total(own_terms, design_ref[...])
    white_obs = total_lanes(own_terms, obs_own[...])
    arrived(halo.at[taps : 2 * taps, :], halo_recv.at[0])
    arrived(halo_obs, halo_recv.at[1])
    first = white[0 : 2 * taps] + total(halo_terms, halo[...])
    obs_first = white_obs[:, 0 : 2 * taps] + total_lanes(halo_terms, halo_obs[:, here - 2 * taps :])
    white = jnp.concatenate([first, white[2 * taps :]], axis=0).T
    white_obs = jnp.concatenate([obs_first, white_obs[:, 2 * taps :]], axis=1)
    mine_lanes = pl.ds(pl.multiple_of(row * here, here), here)
    cols[0:width, mine_lanes] = white.astype(jnp.bfloat16)
    cols[width : width + EXTRA, mine_lanes] = white_obs.astype(jnp.bfloat16)

    def shard(r):
        return cols.at[:, pl.ds(pl.multiple_of(r * here, here), here)]

    def own_part(q):
        return cols.at[pl.ds(pl.multiple_of(q * part, part), part), mine_lanes]

    near_first = [1, 7, 2, 6, 3, 5, 4]
    for i in near_first:
        q = lax.rem(z + i, NZ)
        send(own_part(q), parts.at[z], part_send.at[i], part_recv.at[i], {"z": q})
    own_copy = pltpu.make_async_copy(own_part(z), parts.at[z], part_recv.at[0])
    own_copy.start()

    right_x, left_x = lax.rem(x + 1, NX), lax.rem(x + NX - 1, NX)
    far_x = lax.rem(x + 2, NX)
    partner = x * 2 + 1 - yh
    send(shard(row), shard(row), col_send.at[0], col_recv.at[0], {"yh": 1 - yh})
    send(shard(row), shard(row), col_send.at[1], col_recv.at[1], {"x": right_x})
    send(shard(row), shard(row), col_send.at[2], col_recv.at[2], {"x": left_x})

    conditional = []
    for i in [0] + near_first:
        owner = lax.rem(z + NZ - i, NZ)
        arrived(parts.at[owner], part_recv.at[i])
        target_ref = panel.at[z, mine, :, mine_lanes]
        away = pltpu.make_async_remote_copy(
            src_ref=parts.at[owner], dst_ref=target_ref, send_sem=panel_send.at[i],
            recv_sem=panel_recv.at[row], device_id=at_row(owner), device_id_type=MESH,
        )
        local = pltpu.make_async_copy(parts.at[owner], target_ref, panel_recv.at[row])

        @pl.when(owner != row)
        def _():
            away.start()

        @pl.when(owner == row)
        def _():
            local.start()

        conditional.append((owner, away))

    arrived(shard(partner), col_recv.at[0])
    send(shard(partner), shard(partner), col_send.at[3], col_recv.at[3], {"x": right_x})
    send(shard(partner), shard(partner), col_send.at[4], col_recv.at[4], {"x": left_x})
    from_left = left_x * 2 + yh
    arrived(shard(from_left), col_recv.at[1])
    send(shard(from_left), shard(from_left), col_send.at[5], col_recv.at[5], {"x": right_x})

    F, H = 0, 1
    above, below = {"z": lax.rem(z + 1, NZ)}, {"z": lax.rem(z + NZ - 1, NZ)}
    z_device = (above, below)

    def piece(q, other, h):
        line_of = 1 - yl if other else yl
        return panel.at[q, line_of * 2 + core, :, h * half : (h + 1) * half]

    def halves(q, side):
        start = half + side * quarter
        return panel.at[q, mine, :, start : start + quarter]

    def pass_z(ref, way, d, kind):
        send(ref, ref, z_send.at[way, d, kind], z_recv.at[way, d, kind], z_device[way])

    def pass_lo(ref, slot):
        send(ref, ref, lo_send.at[slot], lo_recv.at[slot], {"yl": 1 - yl})

    def pass_pair(q, o, other, h):
        ref = piece(q, other, h)
        send(ref, ref, pair_send.at[o, other, h], pair_recv.at[o, other, h], {"core": 1 - core})

    def panel_arrived(e):
        arrived(panel.at[z, mine, :, e * here : (e + 1) * here], panel_recv.at[e])

    def group(o):
        q = lax.rem(z + NZ - o, NZ)
        for other in (0, 1):
            for h in (F, H):
                line_of = 1 - yl if other else yl
                arrived(
                    panel.at[q, line_of * 2 + 1 - core, :, h * half : (h + 1) * half],
                    pair_recv.at[o, other, h],
                )
        tile = width // 3

        @pl.loop(0, 3)
        def _(n):
            lanes = pl.ds(pl.multiple_of(n * tile, tile), tile)
            result = lax.dot_general(
                panel[q].reshape(4 * part, deep), cols[lanes, :], by_lane,
                preferred_element_type=jnp.float32,
            )
            out_ref[:, q, :, lanes] = result.reshape(4, part, tile) * (1.0 / deep)

    for e in range(4):
        panel_arrived(e)
    own_f = piece(z, 0, F)
    pass_lo(own_f, NZ)
    pass_z(own_f, UP, 1, 0)
    pass_z(own_f, DOWN, 1, 0)
    pass_pair(z, 0, 0, F)
    for e in range(4, 8):
        panel_arrived(e)
    own_h = piece(z, 0, H)
    pass_z(own_h, UP, 1, 1)
    pass_z(own_h, DOWN, 1, 1)
    pass_lo(own_h, 0)
    pass_pair(z, 0, 0, H)
    other_f = piece(z, 1, F)
    arrived(other_f, lo_recv.at[NZ])
    pass_z(other_f, UP, 1, 2)
    pass_z(other_f, DOWN, 1, 2)
    pass_pair(z, 0, 1, F)

    from_right = right_x * 2 + 1 - yh
    arrived(shard(from_right), col_recv.at[4])
    send(shard(from_right), shard(from_right), col_send.at[6], col_recv.at[6], {"x": left_x})

    def lo_arrived(o):
        q = lax.rem(z + NZ - o, NZ)
        arrived(piece(q, 1, H), lo_recv.at[o])
        pass_pair(q, o, 1, H)

    lo_arrived(0)
    kinds = ((0, F), (0, H), (1, F))

    def hop(d):
        for kind, (other, h) in enumerate(kinds):
            for way in (UP, DOWN):
                o = d if way == UP else NZ - d
                q = lax.rem(z + NZ - o, NZ)
                ref = piece(q, other, h)
                arrived(ref, z_recv.at[way, d, kind])
                if d < 3:
                    pass_z(ref, way, d + 1, kind)
                elif kind == 1:
                    pass_z(halves(q, way), way, d + 1, kind)
                elif kind == (0 if way == UP else 2):
                    pass_z(ref, way, d + 1, kind)
                if kind == 1:
                    pass_lo(ref, o)
                pass_pair(q, o, other, h)
        lo_arrived(d)
        lo_arrived(NZ - d)

    hop(1)
    hop(2)
    arrived(shard(left_x * 2 + 1 - yh), col_recv.at[3])
    arrived(shard(right_x * 2 + yh), col_recv.at[2])
    arrived(shard(far_x * 2 + yh), col_recv.at[5])
    arrived(shard(far_x * 2 + 1 - yh), col_recv.at[6])
    group(0)
    hop(3)
    group(1)
    group(7)
    far = lax.rem(z + 4, NZ)
    for way in (UP, DOWN):
        arrived(halves(far, way), z_recv.at[way, 4, 1])
    pass_lo(piece(far, 0, H), 4)
    pass_pair(far, 4, 0, H)
    group(2)
    group(6)
    arrived(piece(far, 0, F), z_recv.at[UP, 4, 0])
    pass_pair(far, 4, 0, F)
    arrived(piece(far, 1, F), z_recv.at[DOWN, 4, 2])
    pass_pair(far, 4, 1, F)
    right = lax.dot_general(
        cols[width : width + EXTRA, :], cols[0:width, :], by_lane, preferred_element_type=jnp.float32
    )
    right_ref[...] = right * (1.0 / math.sqrt(deep))
    group(3)
    group(5)
    lo_arrived(4)
    group(4)

    for copy in started:
        copy.wait_send()
    for owner, away in conditional:

        @pl.when(owner != row)
        def _():
            away.wait_send()


def on_device(design, observations, filter_taps, tap_count, arc_id):
    here, width = design.shape
    deep = here * ROWS
    part = width // NZ
    vmem = pl.BlockSpec(memory_space=pltpu.VMEM)
    dma = pltpu.SemaphoreType.DMA
    bf16 = jnp.bfloat16
    normal, right = pl.pallas_call(
        body,
        out_shape=(
            jax.ShapeDtypeStruct((4, NZ, part, width), jnp.float32),
            jax.ShapeDtypeStruct((EXTRA, width), jnp.float32),
        ),
        in_specs=[vmem, vmem, vmem, pl.BlockSpec(memory_space=pltpu.SMEM), vmem],
        out_specs=(vmem, vmem),
        scratch_shapes=[
            pltpu.VMEM((width + EXTRA, deep), bf16),
            pltpu.VMEM((NZ, 4, part, deep), bf16),
            pltpu.VMEM((NZ, part, here), bf16),
            pltpu.VMEM((128, width), bf16),
            pltpu.VMEM((EXTRA, here), bf16),
            pltpu.VMEM((EXTRA, here), bf16),
            pltpu.VMEM((8, here), jnp.float32),
            dma((2,)), dma((2,)), dma((NZ,)), dma((NZ,)), dma((1,)), dma((NZ,)), dma((ROWS,)),
            dma((7,)), dma((7,)), dma((2, 5, 3)), dma((2, 5, 3)), dma((9,)), dma((9,)),
            dma((NZ, 2, 2)), dma((NZ, 2, 2)),
        ],
        compiler_params=pltpu.CompilerParams(
            collective_id=0, has_side_effects=True, vmem_limit_bytes=44 * 1024 * 1024
        ),
    )(
        design,
        observations.reshape(1, here),
        filter_taps.reshape(1, -1),
        tap_count,
        arc_id.reshape(ROWS, here),
    )
    return normal.reshape(4 * width, width), right[0]


def solution(mesh):
    finer = Mesh(mesh.devices.reshape(4, 2, 8, 2, 2), AXES)
    row, col = ("x", "yh"), ("z", "yl", "core")
    in_specs = (P(row, col), P(row), P(), P(), P())
    out_specs = (P(row, col), P(col))
    return jax.shard_map(
        on_device, mesh=finer, in_specs=in_specs, out_specs=out_specs, check_vma=False
    )
```

time: 354 us -> 103 us (0.29)
  the two profiles are of different devices: /device:TPU:1 before, /device:TPU:17 now
where the time goes in v1:
time: 103 us
  Pallas kernels  94 us (91%)
  local copies, waits for them, and re-layouts  8.01 us (8%)
    pallas_call x1, Pallas kernels, on_device(): pl.pallas_call(body, out_shape=(jax.ShapeDtypeStruct((4, NZ, part, width)...  94 us
    unnamed x7, local copies, waits for them, and re-layouts  6.05 us

profile of v1, /device:TPU:17, one launch (start us, length us, event | category | flops | bytes accessed | tf_op | source)
XLA Modules:
  0.0 102.7 jit_solution(6575538248456542869)
XLA Ops:
  0.6 0.7 reshape.16.obs_ref
  1.3 0.7 reshape.18.arc_ref
  2.0 0.0 copy-start
  2.0 1.0 copy-done
  3.0 0.0 copy-start.1
  3.0 0.7 copy-done.1
  3.6 0.0 copy-start.2
  3.6 0.7 copy-done.2
  4.3 94.0 %shard_map.68 = (f32[4,8,96,768]{3,2,1,0:T(8,128)S(1)}, f32[16,768]{1,0:T(8,128)S(1)}) custom-call(bf16[256,768]{1,0:T(8,128)(2,1)S(1)} %copy-done, bf16[1,256]{1,0:T(2,128)(2,1)S(1)} %reshape.16.obs_ref, f32[1,64]{1,0:T(1,128)S(1)} %bitcast.3, s32[4]{0:T(128)S(1)} %copy-done.2, s32[8,256]{1,0:T(8,128)S(1)} %reshape.18.arc_ref), custom_call_target="tpu_custom_call" | custom-call | tf_op jit(solution)/shard_map/pallas_call | solution.py:308
  98.3 0.6 slice_reduce_fusion
  99.0 3.7 %copy.8 = f32[3072,768]{1,0:T(8,128)} copy(f32[3072,768]{1,0:T(8,128)S(1)} %bitcast.2) | data formatting | bytes 18874368
Async XLA Ops:
  2.0 1.0 copy-start
  3.0 0.7 copy-start.1
  3.6 0.7 copy-start.2

commit v2 on v1

v2 whole, which is shorter than its diff:
```python
import functools
import math

import jax
import jax.numpy as jnp
from jax import lax
from jax.experimental import pallas as pl
from jax.experimental.pallas import tpu as pltpu
from jax.sharding import Mesh
from jax.sharding import PartitionSpec as P

MESH = pl.DeviceIdType.MESH
AXES = ("x", "yh", "z", "yl", "core")
NX, NZ = 4, 8
ROWS = 8
EXTRA = 16
UP, DOWN = 0, 1


def body(
    taps, arcs, design_ref, table_ref,
    out_ref, right_ref,
    cols, panel, parts, halo, halo_obs, obs_own, table,
    halo_send, halo_recv, part_send, part_recv, panel_send, panel_recv,
    col_send, col_recv, z_send, z_recv, lo_send, lo_recv, pair_send, pair_recv,
):
    x, yh, z = lax.axis_index("x"), lax.axis_index("yh"), lax.axis_index("z")
    yl, core = lax.axis_index("yl"), lax.axis_index("core")
    row = x * 2 + yh
    mine = yl * 2 + core
    here, width = design_ref.shape
    part = width // NZ
    deep = here * ROWS
    half = deep // 2

    def at_row(r):
        return {"x": r // 2, "yh": lax.rem(r, 2)}

    barrier = pltpu.get_barrier_semaphore()
    peers = [at_row(lax.rem(row + i, ROWS)) for i in range(1, ROWS)]
    peers += [{"z": lax.rem(z + i, NZ)} for i in range(1, NZ)]
    peers += [{"yl": 1 - yl}, {"core": 1 - core}]
    for peer in peers:
        pl.semaphore_signal(barrier, inc=1, device_id=peer, device_id_type=MESH)

    table[...] = table_ref[...].reshape(table.shape)
    obs_own[...] = jnp.broadcast_to(table[ROWS : ROWS + 1, :], obs_own.shape).astype(jnp.bfloat16)
    halo[0:taps, :] = jnp.zeros((taps, width), jnp.bfloat16)

    started = []

    def send(src, dst, send_sem, recv_sem, device):
        copy = pltpu.make_async_remote_copy(
            src_ref=src, dst_ref=dst, send_sem=send_sem, recv_sem=recv_sem,
            device_id=device, device_id_type=MESH,
        )
        copy.start()
        started.append(copy)

    def arrived(dst, sem):
        pltpu.make_async_copy(dst, dst, sem).wait()

    line = jnp.broadcast_to(table[ROWS + 1 : ROWS + 2, :], (here, here))
    toeplitz = pltpu.roll(line, 0, 1, stride=1, stride_axis=0).T
    target = lax.broadcasted_iota(jnp.int32, (here, here), 0)
    source = lax.broadcasted_iota(jnp.int32, (here, here), 1)
    lag = target - source
    own = lag >= 0
    lag = jnp.where(own, lag, lag + here)
    arc_here = jnp.broadcast_to(table[pl.ds(row, 1), :], (here, here))
    arc_before = jnp.broadcast_to(table[pl.ds(jnp.maximum(row - 1, 0), 1), :], (here, here))
    arc_before = jnp.where(row > 0, arc_before, -1.0)
    arc_target = arc_here.T
    arc_source = jnp.where(own, arc_here, arc_before)
    limit = jnp.zeros((here, here), jnp.float32)
    for a in range(arcs):
        count = jnp.broadcast_to(table[ROWS + 2 : ROWS + 3, a : a + 1], (here, here))
        limit = jnp.where(arc_target == a, count, limit)
    rows_f = jnp.where(
        (arc_target == arc_source) & (lag.astype(jnp.float32) < limit) & (lag < taps), toeplitz, 0.0
    )

    def three(value):
        high = value.astype(jnp.bfloat16)
        rest = value - high.astype(jnp.float32)
        middle = rest.astype(jnp.bfloat16)
        return high, middle, (rest - middle.astype(jnp.float32)).astype(jnp.bfloat16)

    mid = here // 2
    by_lane = (((1,), (1,)), ((), ()))

    def total(terms, value):
        return sum(jnp.dot(t, value, preferred_element_type=jnp.float32) for t in terms[::-1])

    def total_lanes(terms, value):
        return sum(
            lax.dot_general(value, t, by_lane, preferred_element_type=jnp.float32) for t in terms[::-1]
        )

    F, H = 0, 1

    def lanes_of(r, h):
        return pl.ds(pl.multiple_of(h * half + r * mid, mid), mid)

    late = three(rows_f[mid:, :])
    cols[0:width, lanes_of(row, F)] = total(late, design_ref[...]).T.astype(jnp.bfloat16)
    cols[width : width + EXTRA, lanes_of(row, F)] = total_lanes(late, obs_own[...]).astype(jnp.bfloat16)
    early = three(jnp.where(own, rows_f, 0.0)[0:mid, 0:mid])
    before = three(jnp.where(own, 0.0, rows_f)[0:mid, here - 2 * taps :])

    def shard(r, h):
        return cols.at[:, lanes_of(r, h)]

    def own_part(q, h):
        return cols.at[pl.ds(pl.multiple_of(q * part, part), part), lanes_of(row, h)]

    right_x, left_x = lax.rem(x + 1, NX), lax.rem(x + NX - 1, NX)
    far_x = lax.rem(x + 2, NX)
    partner = x * 2 + 1 - yh
    near_first = [1, 7, 2, 6, 3, 5, 4]

    def pass_parts(h):
        for i in near_first:
            q = lax.rem(z + i, NZ)
            send(own_part(q, h), parts.at[h, z], part_send.at[h, i], part_recv.at[h, i], {"z": q})

    def pass_col(r, h, slot, device):
        send(shard(r, h), shard(r, h), col_send.at[h, slot], col_recv.at[h, slot], device)

    def col_arrived(r, h, slot):
        arrived(shard(r, h), col_recv.at[h, slot])

    def col_own(h):
        pass_col(row, h, 0, {"yh": 1 - yh})
        pass_col(row, h, 1, {"x": right_x})
        pass_col(row, h, 2, {"x": left_x})

    def col_first(h):
        col_arrived(partner, h, 0)
        pass_col(partner, h, 3, {"x": right_x})
        pass_col(partner, h, 4, {"x": left_x})
        col_arrived(left_x * 2 + yh, h, 1)
        pass_col(left_x * 2 + yh, h, 5, {"x": right_x})

    def col_second(h):
        col_arrived(right_x * 2 + 1 - yh, h, 4)
        pass_col(right_x * 2 + 1 - yh, h, 6, {"x": left_x})

    def col_last(h):
        col_arrived(left_x * 2 + 1 - yh, h, 3)
        col_arrived(right_x * 2 + yh, h, 2)
        col_arrived(far_x * 2 + yh, h, 5)
        col_arrived(far_x * 2 + 1 - yh, h, 6)

    conditional = []

    def pass_rows(h):
        for i in [0] + near_first:
            owner = lax.rem(z + NZ - i, NZ)
            source = parts.at[h, owner]
            if i == 0:
                source = own_part(z, h)
            else:
                arrived(source, part_recv.at[h, i])
            target_ref = panel.at[z, mine, :, lanes_of(row, h)]
            away = pltpu.make_async_remote_copy(
                src_ref=source, dst_ref=target_ref, send_sem=panel_send.at[h, i],
                recv_sem=panel_recv.at[h, row], device_id=at_row(owner), device_id_type=MESH,
            )
            local = pltpu.make_async_copy(source, target_ref, panel_recv.at[h, row])

            @pl.when(owner != row)
            def _():
                away.start()

            @pl.when(owner == row)
            def _():
                local.start()

            conditional.append((owner, away))

    above, below = {"z": lax.rem(z + 1, NZ)}, {"z": lax.rem(z + NZ - 1, NZ)}
    z_device = (above, below)

    def piece(q, other, h, other_core=False):
        line_of = 1 - yl if other else yl
        core_of = 1 - core if other_core else core
        return panel.at[q, line_of * 2 + core_of, :, h * half : (h + 1) * half]

    def halves(q, side):
        return panel.at[q, mine, side * (part // 2) : (side + 1) * (part // 2), half:deep]

    def pass_z(ref, way, d, kind):
        send(ref, ref, z_send.at[way, d, kind], z_recv.at[way, d, kind], z_device[way])

    def pass_lo(ref, slot):
        send(ref, ref, lo_send.at[slot], lo_recv.at[slot], {"yl": 1 - yl})

    def pass_pair(q, o, other, h):
        ref = piece(q, other, h)
        send(ref, ref, pair_send.at[o, other, h], pair_recv.at[o, other, h], {"core": 1 - core})

    def panel_arrived(h):
        for e in range(ROWS):
            start = h * half + e * mid
            arrived(panel.at[z, mine, :, start : start + mid], panel_recv.at[h, e])

    def group(o):
        q = lax.rem(z + NZ - o, NZ)
        for other in (0, 1):
            for h in (F, H):
                arrived(piece(q, other, h, True), pair_recv.at[o, other, h])
        tile = width // 3

        @pl.loop(0, 3)
        def _(n):
            lanes = pl.ds(pl.multiple_of(n * tile, tile), tile)
            result = lax.dot_general(
                panel[q].reshape(4 * part, deep), cols[lanes, :], by_lane,
                preferred_element_type=jnp.float32,
            )
            out_ref[:, q, :, lanes] = result.reshape(4, part, tile) * (1.0 / deep)

    def lo_arrived(o):
        q = lax.rem(z + NZ - o, NZ)
        arrived(piece(q, 1, H), lo_recv.at[o])
        pass_pair(q, o, 1, H)

    kinds = ((0, F), (0, H), (1, F))

    def hop(d, kind):
        other, h = kinds[kind]
        for way in (UP, DOWN):
            o = d if way == UP else NZ - d
            q = lax.rem(z + NZ - o, NZ)
            ref = piece(q, other, h)
            arrived(ref, z_recv.at[way, d, kind])
            if d < 3:
                pass_z(ref, way, d + 1, kind)
            elif kind == 1:
                pass_z(halves(q, way), way, d + 1, kind)
            elif kind == (0 if way == UP else 2):
                pass_z(ref, way, d + 1, kind)
            if kind == 1:
                pass_lo(ref, o)
            pass_pair(q, o, other, h)

    pl.semaphore_wait(barrier, len(peers))
    after = at_row(lax.rem(row + 1, ROWS))
    send(design_ref.at[here - taps : here, :], halo.at[taps : 2 * taps, :], halo_send.at[0], halo_recv.at[0], after)
    send(obs_own, halo_obs, halo_send.at[1], halo_recv.at[1], after)
    pass_parts(F)
    col_own(F)

    arrived(halo.at[taps : 2 * taps, :], halo_recv.at[0])
    arrived(halo_obs, halo_recv.at[1])
    white = total(early, design_ref[0:mid, :]) + total(before, halo[...])
    cols[0:width, lanes_of(row, H)] = white.T.astype(jnp.bfloat16)
    obs_white = total_lanes(early, obs_own[:, 0:mid]) + total_lanes(before, halo_obs[:, here - 2 * taps :])
    cols[width : width + EXTRA, lanes_of(row, H)] = obs_white.astype(jnp.bfloat16)
    pass_parts(H)
    pass_rows(F)
    pass_rows(H)
    col_own(H)
    panel_arrived(F)
    own_f = piece(z, 0, F)
    pass_lo(own_f, NZ)
    pass_z(own_f, UP, 1, 0)
    pass_z(own_f, DOWN, 1, 0)
    pass_pair(z, 0, 0, F)
    panel_arrived(H)
    own_h = piece(z, 0, H)
    pass_z(own_h, UP, 1, 1)
    pass_z(own_h, DOWN, 1, 1)
    pass_lo(own_h, 0)
    pass_pair(z, 0, 0, H)

    other_f = piece(z, 1, F)
    arrived(other_f, lo_recv.at[NZ])
    pass_z(other_f, UP, 1, 2)
    pass_z(other_f, DOWN, 1, 2)
    pass_pair(z, 0, 1, F)
    col_first(F)

    hop(1, 0)
    col_first(H)
    hop(1, 1)
    col_second(F)
    lo_arrived(0)
    hop(1, 2)
    col_second(H)
    hop(2, 0)
    lo_arrived(1)
    hop(2, 1)
    lo_arrived(7)
    hop(2, 2)
    col_last(F)
    col_last(H)
    group(0)
    group(1)
    hop(3, 1)
    group(7)
    hop(3, 0)
    lo_arrived(2)
    group(2)
    hop(3, 2)
    lo_arrived(6)
    group(6)
    far = lax.rem(z + 4, NZ)
    for way in (UP, DOWN):
        arrived(halves(far, way), z_recv.at[way, 4, 1])
    pass_lo(piece(far, 0, H), 4)
    pass_pair(far, 4, 0, H)
    lo_arrived(3)
    lo_arrived(5)
    right = lax.dot_general(
        cols[width : width + EXTRA, :], cols[0:width, :], by_lane, preferred_element_type=jnp.float32
    )
    right_ref[...] = right * (1.0 / math.sqrt(deep))
    group(3)
    arrived(piece(far, 0, F), z_recv.at[UP, 4, 0])
    pass_pair(far, 4, 0, F)
    arrived(piece(far, 1, F), z_recv.at[DOWN, 4, 2])
    pass_pair(far, 4, 1, F)
    group(5)
    lo_arrived(4)
    group(4)

    for copy in started:
        copy.wait_send()
    for owner, away in conditional:

        @pl.when(owner != row)
        def _():
            away.wait_send()


def on_device(design, observations, filter_taps, tap_count, arc_id):
    here, width = design.shape
    taps, arcs = filter_taps.shape[0], tap_count.shape[0]
    deep = here * ROWS
    part = width // NZ
    vmem = pl.BlockSpec(memory_space=pltpu.VMEM)
    dma = pltpu.SemaphoreType.DMA
    bf16, f32 = jnp.bfloat16, jnp.float32
    table = jnp.concatenate(
        [
            arc_id.astype(f32),
            observations.astype(f32),
            jnp.pad(filter_taps, (0, here - taps)),
            jnp.pad(tap_count.astype(f32), (0, 6 * here - arcs)),
        ]
    )
    normal, right = pl.pallas_call(
        functools.partial(body, taps, arcs),
        out_shape=(
            jax.ShapeDtypeStruct((4, NZ, part, width), f32),
            jax.ShapeDtypeStruct((EXTRA, width), f32),
        ),
        in_specs=[vmem, vmem],
        out_specs=(vmem, vmem),
        scratch_shapes=[
            pltpu.VMEM((width + EXTRA, deep), bf16),
            pltpu.VMEM((NZ, 4, part, deep), bf16),
            pltpu.VMEM((2, NZ, part, here // 2), bf16),
            pltpu.VMEM((2 * taps, width), bf16),
            pltpu.VMEM((EXTRA, here), bf16),
            pltpu.VMEM((EXTRA, here), bf16),
            pltpu.VMEM((16, here), f32),
            dma((2,)), dma((2,)), dma((2, NZ)), dma((2, NZ)), dma((2, NZ)), dma((2, ROWS)),
            dma((2, 7)), dma((2, 7)), dma((2, 5, 3)), dma((2, 5, 3)), dma((9,)), dma((9,)),
            dma((NZ, 2, 2)), dma((NZ, 2, 2)),
        ],
        compiler_params=pltpu.CompilerParams(
            collective_id=0, has_side_effects=True, vmem_limit_bytes=44 * 1024 * 1024
        ),
    )(design, table)
    return normal.reshape(4 * width, width), right[0]


def solution(mesh):
    finer = Mesh(mesh.devices.reshape(4, 2, 8, 2, 2), AXES)
    row, col = ("x", "yh"), ("z", "yl", "core")
    in_specs = (P(row, col), P(row), P(), P(), P())
    out_specs = (P(row, col), P(col))
    return jax.shard_map(
        on_device, mesh=finer, in_specs=in_specs, out_specs=out_specs, check_vma=False
    )
```

time: 103 us -> 90.8 us (0.88)
  the two profiles are of different devices: /device:TPU:17 before, /device:TPU:1 now
where the time goes in v2:
time: 90.8 us; the launch traced here: 90.6 us
  Pallas kernels  82 us (90%)
  local copies, waits for them, and re-layouts  5.34 us (6%)
  other arithmetic  2.68 us (3%)
    pallas_call x1, Pallas kernels, on_device(): pl.pallas_call(functools.partial(body, taps, arcs), out_shape=(jax.ShapeD...  82 us
    unnamed x3, local copies, waits for them, and re-layouts  4.74 us

profile of v2, /device:TPU:1, one launch (start us, length us, event | category | flops | bytes accessed | tf_op | source)
XLA Modules:
  0.0 90.6 jit_solution(15044422510982734005)
XLA Ops:
  0.6 0.7 convert_element_type.15
  1.3 0.7 convert_element_type.14
  1.9 0.7 convert_element_type.13
  2.6 0.7 select_maximum_fusion.table_ref
  3.3 0.0 copy-start
  3.3 1.0 %copy-done = bf16[256,768]{1,0:T(8,128)(2,1)S(1)} copy-done((bf16[256,768]{1,0:T(8,128)(2,1)S(1)}, bf16[256,768]{1,0:T(8,128)(2,1)}, u32[]{:S(2)}) %copy-start) | copy-done | bytes 393240
  4.3 82.0 %shard_map.68 = (f32[4,8,96,768]{3,2,1,0:T(8,128)S(1)}, f32[16,768]{1,0:T(8,128)S(1)}) custom-call(bf16[256,768]{1,0:T(8,128)(2,1)S(1)} %copy-done, f32[4096]{0:T(1024)S(1)} %select_maximum_fusion.table_ref), custom_call_target="tpu_custom_call" | custom-call | tf_op jit(solution)/shard_map/pallas_call | solution.py:354
  86.3 0.6 slice_reduce_fusion
  86.9 3.7 %copy.8 = f32[3072,768]{1,0:T(8,128)} copy(f32[3072,768]{1,0:T(8,128)S(1)} %bitcast.1) | data formatting | bytes 18874368
Async XLA Ops:
  3.3 1.0 %copy-start = (bf16[256,768]{1,0:T(8,128)(2,1)S(1)}, bf16[256,768]{1,0:T(8,128)(2,1)}, u32[]{:S(2)}) copy-start(bf16[256,768]{1,0:T(8,128)(2,1)} %design_ref.1) | copy-start | bytes 1179652

commit v3 on v2

--- a/solution.py
+++ b/solution.py
@@ -10,17 +10,62 @@
 from jax.sharding import PartitionSpec as P
 
 MESH = pl.DeviceIdType.MESH
+LIMIT1, LIMIT2 = 28, 28
 AXES = ("x", "yh", "z", "yl", "core")
 NX, NZ = 4, 8
 ROWS = 8
 EXTRA = 16
 UP, DOWN = 0, 1
 
+LATER = (5, 4)
+EARLY = 80
+LATE_SIDES = (0,)
+BY_LANE = (((1,), (1,)), ((), ()))
+
+
+def multiply(panel, cols, out_ref, q, slot):
+    _, lines, part, deep = panel.shape
+    width = out_ref.shape[-1]
+    tile = width // 3
+
+    @pl.loop(0, 3)
+    def _(n):
+        lanes = pl.ds(pl.multiple_of(n * tile, tile), tile)
+        result = lax.dot_general(
+            panel[q].reshape(lines * part, deep), cols[lanes, :], BY_LANE, preferred_element_type=jnp.float32
+        )
+        out_ref[:, slot, :, lanes] = result.reshape(lines, part, tile) * (1.0 / deep)
+
+
+def finish(done, cols, panel, out_ref, right_ref, last, sems):
+    width = done.shape[-1]
+    deep = panel.shape[-1]
+    z = lax.axis_index("z")
+    copies = []
+
+    def write(source, q):
+        copy = pltpu.make_async_copy(source, out_ref.at[:, q], sems.at[len(copies)])
+        copy.start()
+        copies.append(copy)
+
+    for o in range(NZ):
+        q = lax.rem(z + NZ - o, NZ)
+        if o not in LATER:
+            write(done.at[:, q], q)
+    for slot, o in enumerate(LATER):
+        q = lax.rem(z + NZ - o, NZ)
+        multiply(panel, cols, last, q, slot)
+        write(last.at[:, slot], q)
+    right = lax.dot_general(cols[width:, :], cols[0:width, :], BY_LANE, preferred_element_type=jnp.float32)
+    right_ref[...] = right[0:1, :].reshape(width) * (1.0 / math.sqrt(deep))
+    for copy in copies:
+        copy.wait()
+
 
 def body(
     taps, arcs, design_ref, table_ref,
-    out_ref, right_ref,
-    cols, panel, parts, halo, halo_obs, obs_own, table,
+    out_ref, cols, panel,
+    parts, halo, halo_obs, obs_own, table,
     halo_send, halo_recv, part_send, part_recv, panel_send, panel_recv,
     col_send, col_recv, z_send, z_recv, lo_send, lo_recv, pair_send, pair_recv,
 ):
@@ -97,14 +142,14 @@
             lax.dot_general(value, t, by_lane, preferred_element_type=jnp.float32) for t in terms[::-1]
         )
 
-    F, H = 0, 1
+    H, F = 0, 1
 
     def lanes_of(r, h):
         return pl.ds(pl.multiple_of(h * half + r * mid, mid), mid)
 
     late = three(rows_f[mid:, :])
-    cols[0:width, lanes_of(row, F)] = total(late, design_ref[...]).T.astype(jnp.bfloat16)
-    cols[width : width + EXTRA, lanes_of(row, F)] = total_lanes(late, obs_own[...]).astype(jnp.bfloat16)
+    cols[0:width, lanes_of(row, H)] = total(late, design_ref[...]).T.astype(jnp.bfloat16)
+    cols[width : width + EXTRA, lanes_of(row, H)] = total_lanes(late, obs_own[...]).astype(jnp.bfloat16)
     early = three(jnp.where(own, rows_f, 0.0)[0:mid, 0:mid])
     before = three(jnp.where(own, 0.0, rows_f)[0:mid, here - 2 * taps :])
 
@@ -130,8 +175,10 @@
     def col_arrived(r, h, slot):
         arrived(shard(r, h), col_recv.at[h, slot])
 
-    def col_own(h):
+    def col_y(h):
         pass_col(row, h, 0, {"yh": 1 - yh})
+
+    def col_x(h):
         pass_col(row, h, 1, {"x": right_x})
         pass_col(row, h, 2, {"x": left_x})
 
@@ -188,7 +235,20 @@
         return panel.at[q, line_of * 2 + core_of, :, h * half : (h + 1) * half]
 
     def halves(q, side):
-        return panel.at[q, mine, side * (part // 2) : (side + 1) * (part // 2), half:deep]
+        return panel.at[q, mine, side * (part // 2) : (side + 1) * (part // 2), 0:half]
+
+    def early_rows(q, other):
+        line_of = 1 - yl if other else yl
+        return panel.at[q, line_of * 2 + core, 0:EARLY, half:deep]
+
+    def late_rows(q, other):
+        line_of = 1 - yl if other else yl
+        return panel.at[q, line_of * 2 + core, EARLY:part, half:deep]
+
+    def late_side(q, side):
+        cut = EARLY + (part - EARLY) // 2 if len(LATE_SIDES) == 2 else part
+        start, stop = (EARLY, cut) if side == UP else (cut, part)
+        return panel.at[q, mine, start:stop, half:deep]
 
     def pass_z(ref, way, d, kind):
         send(ref, ref, z_send.at[way, d, kind], z_recv.at[way, d, kind], z_device[way])
@@ -210,118 +270,127 @@
         for other in (0, 1):
             for h in (F, H):
                 arrived(piece(q, other, h, True), pair_recv.at[o, other, h])
-        tile = width // 3
-
-        @pl.loop(0, 3)
-        def _(n):
-            lanes = pl.ds(pl.multiple_of(n * tile, tile), tile)
-            result = lax.dot_general(
-                panel[q].reshape(4 * part, deep), cols[lanes, :], by_lane,
-                preferred_element_type=jnp.float32,
-            )
-            out_ref[:, q, :, lanes] = result.reshape(4, part, tile) * (1.0 / deep)
+        if o not in LATER:
+            multiply(panel, cols, out_ref, q, q)
 
     def lo_arrived(o):
         q = lax.rem(z + NZ - o, NZ)
         arrived(piece(q, 1, H), lo_recv.at[o])
         pass_pair(q, o, 1, H)
-
-    kinds = ((0, F), (0, H), (1, F))
+        arrived(late_rows(q, 1), lo_recv.at[NZ + 1 + o])
+        pass_pair(q, o, 1, F)
+
+    EARLY_OWN, LATE, HALF, EARLY_OTHER = 0, 1, 2, 3
+
+    def ref_of(q, kind):
+        if kind == EARLY_OWN:
+            return early_rows(q, 0)
+        if kind == LATE:
+            return late_rows(q, 0)
+        if kind == HALF:
+            return piece(q, 0, H)
+        return early_rows(q, 1)
+
+    def onward(q, o, kind):
+        if kind == LATE:
+            pass_lo(late_rows(q, 0), NZ + 1 + o)
+        elif kind == HALF:
+            pass_lo(piece(q, 0, H), o)
+            pass_pair(q, o, 0, H)
+        elif kind == EARLY_OWN:
+            pass_pair(q, o, 0, F)
 
     def hop(d, kind):
-        other, h = kinds[kind]
         for way in (UP, DOWN):
             o = d if way == UP else NZ - d
             q = lax.rem(z + NZ - o, NZ)
-            ref = piece(q, other, h)
+            ref = ref_of(q, kind)
             arrived(ref, z_recv.at[way, d, kind])
             if d < 3:
                 pass_z(ref, way, d + 1, kind)
-            elif kind == 1:
+            elif kind == HALF:
                 pass_z(halves(q, way), way, d + 1, kind)
-            elif kind == (0 if way == UP else 2):
+            elif kind == LATE and way in LATE_SIDES:
+                pass_z(late_side(q, way), way, d + 1, kind)
+            elif kind == (EARLY_OWN if way == UP else EARLY_OTHER):
                 pass_z(ref, way, d + 1, kind)
-            if kind == 1:
-                pass_lo(ref, o)
-            pass_pair(q, o, other, h)
+            onward(q, o, kind)
 
     pl.semaphore_wait(barrier, len(peers))
     after = at_row(lax.rem(row + 1, ROWS))
     send(design_ref.at[here - taps : here, :], halo.at[taps : 2 * taps, :], halo_send.at[0], halo_recv.at[0], after)
     send(obs_own, halo_obs, halo_send.at[1], halo_recv.at[1], after)
-    pass_parts(F)
-    col_own(F)
+    pass_parts(H)
+    col_y(H)
+    col_x(H)
 
     arrived(halo.at[taps : 2 * taps, :], halo_recv.at[0])
     arrived(halo_obs, halo_recv.at[1])
     white = total(early, design_ref[0:mid, :]) + total(before, halo[...])
-    cols[0:width, lanes_of(row, H)] = white.T.astype(jnp.bfloat16)
+    cols[0:width, lanes_of(row, F)] = white.T.astype(jnp.bfloat16)
     obs_white = total_lanes(early, obs_own[:, 0:mid]) + total_lanes(before, halo_obs[:, here - 2 * taps :])
-    cols[width : width + EXTRA, lanes_of(row, H)] = obs_white.astype(jnp.bfloat16)
-    pass_parts(H)
+    cols[width : width + EXTRA, lanes_of(row, F)] = obs_white.astype(jnp.bfloat16)
+    pass_parts(F)
+    pass_rows(H)
     pass_rows(F)
-    pass_rows(H)
-    col_own(H)
+    col_x(F)
+    panel_arrived(H)
+    pass_lo(piece(z, 0, H), 0)
+    pass_z(ref_of(z, HALF), UP, 1, HALF)
+    pass_z(ref_of(z, HALF), DOWN, 1, HALF)
+    pass_pair(z, 0, 0, H)
     panel_arrived(F)
-    own_f = piece(z, 0, F)
-    pass_lo(own_f, NZ)
-    pass_z(own_f, UP, 1, 0)
-    pass_z(own_f, DOWN, 1, 0)
-    pass_pair(z, 0, 0, F)
-    panel_arrived(H)
-    own_h = piece(z, 0, H)
-    pass_z(own_h, UP, 1, 1)
-    pass_z(own_h, DOWN, 1, 1)
-    pass_lo(own_h, 0)
-    pass_pair(z, 0, 0, H)
-
-    other_f = piece(z, 1, F)
-    arrived(other_f, lo_recv.at[NZ])
-    pass_z(other_f, UP, 1, 2)
-    pass_z(other_f, DOWN, 1, 2)
-    pass_pair(z, 0, 1, F)
+    pass_lo(early_rows(z, 0), NZ)
+    for kind in (LATE, EARLY_OWN):
+        pass_z(ref_of(z, kind), UP, 1, kind)
+        pass_z(ref_of(z, kind), DOWN, 1, kind)
+        onward(z, 0, kind)
+    col_y(F)
+    col_first(H)
+    arrived(early_rows(z, 1), lo_recv.at[NZ])
+    pass_z(early_rows(z, 1), UP, 1, EARLY_OTHER)
+    pass_z(early_rows(z, 1), DOWN, 1, EARLY_OTHER)
+
+    hop(1, HALF)
+    hop(1, LATE)
+    hop(1, EARLY_OWN)
+    col_second(H)
+    hop(1, EARLY_OTHER)
     col_first(F)
-
-    hop(1, 0)
-    col_first(H)
-    hop(1, 1)
+    lo_arrived(0)
+    hop(2, HALF)
+    lo_arrived(1)
+    hop(2, LATE)
+    hop(2, EARLY_OWN)
+    lo_arrived(7)
     col_second(F)
-    lo_arrived(0)
-    hop(1, 2)
-    col_second(H)
-    hop(2, 0)
-    lo_arrived(1)
-    hop(2, 1)
-    lo_arrived(7)
-    hop(2, 2)
+    hop(2, EARLY_OTHER)
+    hop(3, HALF)
+    col_last(H)
     col_last(F)
-    col_last(H)
     group(0)
+    hop(3, LATE)
     group(1)
-    hop(3, 1)
+    hop(3, EARLY_OWN)
+    lo_arrived(2)
     group(7)
-    hop(3, 0)
-    lo_arrived(2)
+    hop(3, EARLY_OTHER)
+    lo_arrived(6)
     group(2)
-    hop(3, 2)
-    lo_arrived(6)
-    group(6)
     far = lax.rem(z + 4, NZ)
     for way in (UP, DOWN):
-        arrived(halves(far, way), z_recv.at[way, 4, 1])
-    pass_lo(piece(far, 0, H), 4)
-    pass_pair(far, 4, 0, H)
+        arrived(halves(far, way), z_recv.at[way, 4, HALF])
+    onward(far, 4, HALF)
+    for way in LATE_SIDES:
+        arrived(late_side(far, way), z_recv.at[way, 4, LATE])
+    onward(far, 4, LATE)
+    group(6)
     lo_arrived(3)
     lo_arrived(5)
-    right = lax.dot_general(
-        cols[width : width + EXTRA, :], cols[0:width, :], by_lane, preferred_element_type=jnp.float32
-    )
-    right_ref[...] = right * (1.0 / math.sqrt(deep))
     group(3)
-    arrived(piece(far, 0, F), z_recv.at[UP, 4, 0])
-    pass_pair(far, 4, 0, F)
-    arrived(piece(far, 1, F), z_recv.at[DOWN, 4, 2])
-    pass_pair(far, 4, 1, F)
+    arrived(early_rows(far, 0), z_recv.at[UP, 4, EARLY_OWN])
+    onward(far, 4, EARLY_OWN)
+    arrived(early_rows(far, 1), z_recv.at[DOWN, 4, EARLY_OTHER])
     group(5)
     lo_arrived(4)
     group(4)
@@ -343,39 +412,47 @@
     vmem = pl.BlockSpec(memory_space=pltpu.VMEM)
     dma = pltpu.SemaphoreType.DMA
     bf16, f32 = jnp.bfloat16, jnp.float32
-    table = jnp.concatenate(
-        [
-            arc_id.astype(f32),
-            observations.astype(f32),
-            jnp.pad(filter_taps, (0, here - taps)),
-            jnp.pad(tap_count.astype(f32), (0, 6 * here - arcs)),
-        ]
-    )
-    normal, right = pl.pallas_call(
+    whole = 16 * here
+
+    def spread(value, start):
+        return jnp.pad(value, (start, whole - start - value.shape[0])).astype(f32)
+
+    table = spread(arc_id, 0) + spread(observations, deep) + spread(filter_taps, deep + here) + spread(tap_count, deep + 2 * here)
+    done, cols, panel = pl.pallas_call(
         functools.partial(body, taps, arcs),
         out_shape=(
             jax.ShapeDtypeStruct((4, NZ, part, width), f32),
-            jax.ShapeDtypeStruct((EXTRA, width), f32),
+            jax.ShapeDtypeStruct((width + EXTRA, deep), bf16),
+            jax.ShapeDtypeStruct((NZ, 4, part, deep), bf16),
         ),
         in_specs=[vmem, vmem],
-        out_specs=(vmem, vmem),
+        out_specs=(vmem, vmem, vmem),
         scratch_shapes=[
-            pltpu.VMEM((width + EXTRA, deep), bf16),
-            pltpu.VMEM((NZ, 4, part, deep), bf16),
             pltpu.VMEM((2, NZ, part, here // 2), bf16),
             pltpu.VMEM((2 * taps, width), bf16),
             pltpu.VMEM((EXTRA, here), bf16),
             pltpu.VMEM((EXTRA, here), bf16),
             pltpu.VMEM((16, here), f32),
             dma((2,)), dma((2,)), dma((2, NZ)), dma((2, NZ)), dma((2, NZ)), dma((2, ROWS)),
-            dma((2, 7)), dma((2, 7)), dma((2, 5, 3)), dma((2, 5, 3)), dma((9,)), dma((9,)),
+            dma((2, 7)), dma((2, 7)), dma((2, 5, 4)), dma((2, 5, 4)), dma((17,)), dma((17,)),
             dma((NZ, 2, 2)), dma((NZ, 2, 2)),
         ],
         compiler_params=pltpu.CompilerParams(
-            collective_id=0, has_side_effects=True, vmem_limit_bytes=44 * 1024 * 1024
+            collective_id=0, has_side_effects=True, vmem_limit_bytes=LIMIT1 * 1024 * 1024
         ),
     )(design, table)
-    return normal.reshape(4 * width, width), right[0]
+    normal, right = pl.pallas_call(
+        finish,
+        out_shape=(
+            jax.ShapeDtypeStruct((4, NZ, part, width), f32),
+            jax.ShapeDtypeStruct((width,), f32),
+        ),
+        in_specs=[vmem, vmem, vmem],
+        out_specs=(pl.BlockSpec(memory_space=pl.ANY), vmem),
+        scratch_shapes=[pltpu.VMEM((4, len(LATER), part, width), f32), dma((NZ,))],
+        compiler_params=pltpu.CompilerParams(vmem_limit_bytes=LIMIT2 * 1024 * 1024),
+    )(done, cols, panel)
+    return normal.reshape(4 * width, width), right
 
 
 def solution(mesh):

time: 90.8 us -> 84.6 us (0.932)
  local copies, waits for them, and re-layouts: 5.34 us -> 0.99 us
  other arithmetic: 2.68 us -> 0.74 us
    pallas_call x0 -> x1, Pallas kernels: none -> 5.35 us  [on_device(): pl.pallas_call(finish, out_shape=(jax.ShapeDtypeStruct((4, NZ, part, widt...]
    pallas_call x1, Pallas kernels: 82 us -> 76.8 us  [on_device(): pl.pallas_call(functools.partial(body, taps, arcs), out_shape=(jax.ShapeD...]
    unnamed x3 -> x2, local copies, waits for them, and re-layouts: 4.74 us -> 0.99 us
    convert_element_type x3 -> x0, other arithmetic: 2.01 us -> none  [the longest x1 0.7 us: on_device(): arc_id.astype(f32)]
where the time goes in v3:
time: 84.6 us; the launch traced here: 84.5 us
  Pallas kernels  82.1 us (97%)
  local copies, waits for them, and re-layouts  0.99 us (1%)
    pallas_call x1, Pallas kernels, on_device(): pl.pallas_call(functools.partial(body, taps, arcs), out_shape=(jax.ShapeD...  76.8 us
    pallas_call x1, Pallas kernels, on_device(): pl.pallas_call(finish, out_shape=(jax.ShapeDtypeStruct((4, NZ, part, widt...  5.35 us

profile of v3, /device:TPU:1, one launch (start us, length us, event | category | flops | bytes accessed | tf_op | source)
XLA Modules:
  0.0 84.5 jit_solution(9097789275873346802)
XLA Ops:
  0.6 0.7 convert_add_fusion.table_ref
  1.4 0.0 copy-start
  1.4 1.0 %copy-done = bf16[256,768]{1,0:T(8,128)(2,1)S(1)} copy-done((bf16[256,768]{1,0:T(8,128)(2,1)S(1)}, bf16[256,768]{1,0:T(8,128)(2,1)}, u32[]{:S(2)}) %copy-start) | copy-done | bytes 393240
  2.4 76.8 %shard_map.68 = (f32[4,8,96,768]{3,2,1,0:T(8,128)S(1)}, bf16[784,2048]{1,0:T(8,128)(2,1)S(1)}, bf16[8,4,96,2048]{3,2,1,0:T(8,128)(2,1)S(1)}) custom-call(bf16[256,768]{1,0:T(8,128)(2,1)S(1)} %copy-done, f32[4096]{0:T(1024)S(1)} %convert_add_fusion.table_ref), custom_call_target="tpu_custom_call" | custom-call | tf_op jit(solution)/shard_map/pallas_call | solution.py:421
  79.1 5.4 %shard_map.69 = (f32[4,8,96,768]{3,2,1,0:T(8,128)}, f32[768]{0:T(1024)}) custom-call(f32[4,8,96,768]{3,2,1,0:T(8,128)S(1)} %get-tuple-element.7.done, bf16[784,2048]{1,0:T(8,128)(2,1)S(1)} %get-tuple-element.8.cols, bf16[8,4,96,2048]{3,2,1,0:T(8,128)(2,1)S(1)} %get-tuple-element.9.panel), custom_call_target="tpu_custom_call" | custom-call | tf_op jit(solution)/shard_map/pallas_call | solution.py:444
Async XLA Ops:
  1.4 1.0 %copy-start = (bf16[256,768]{1,0:T(8,128)(2,1)S(1)}, bf16[256,768]{1,0:T(8,128)(2,1)}, u32[]{:S(2)}) copy-start(bf16[256,768]{1,0:T(8,128)(2,1)} %design_ref.1) | copy-start | bytes 1179652

commit v4 on v3

--- a/solution.py
+++ b/solution.py
@@ -17,7 +17,7 @@
 EXTRA = 16
 UP, DOWN = 0, 1
 
-LATER = (5, 4)
+LATER = (4,)
 EARLY = 80
 LATE_SIDES = (0,)
 BY_LANE = (((1,), (1,)), ((), ()))
@@ -37,7 +37,7 @@
         out_ref[:, slot, :, lanes] = result.reshape(lines, part, tile) * (1.0 / deep)
 
 
-def finish(done, cols, panel, out_ref, right_ref, last, sems):
+def finish(done, cols, panel, out_ref, right_ref, last, sems, tile_sems):
     width = done.shape[-1]
     deep = panel.shape[-1]
     z = lax.axis_index("z")
@@ -52,14 +52,34 @@
         q = lax.rem(z + NZ - o, NZ)
         if o not in LATER:
             write(done.at[:, q], q)
-    for slot, o in enumerate(LATER):
-        q = lax.rem(z + NZ - o, NZ)
-        multiply(panel, cols, last, q, slot)
-        write(last.at[:, slot], q)
+    tiles = 3
+    tile = width // tiles
+
+    def tile_copy(t):
+        slot, n = t // tiles, lax.rem(t, tiles)
+        q = lax.rem(z + NZ - LATER[0] + slot, NZ)
+        lanes = pl.ds(pl.multiple_of(n * tile, tile), tile)
+        return q, slot, lanes, pltpu.make_async_copy(
+            last.at[:, slot, :, lanes], out_ref.at[:, q, :, lanes], tile_sems.at[t]
+        )
+
+    @pl.loop(0, tiles * len(LATER))
+    def _(t):
+        q, slot, lanes, copy = tile_copy(t)
+        result = lax.dot_general(
+            panel[q].reshape(-1, deep), cols[lanes, :], BY_LANE, preferred_element_type=jnp.float32
+        )
+        last[:, slot, :, lanes] = result.reshape(last.shape[0], -1, tile) * (1.0 / deep)
+        copy.start()
+
     right = lax.dot_general(cols[width:, :], cols[0:width, :], BY_LANE, preferred_element_type=jnp.float32)
     right_ref[...] = right[0:1, :].reshape(width) * (1.0 / math.sqrt(deep))
     for copy in copies:
         copy.wait()
+
+    @pl.loop(0, tiles * len(LATER))
+    def _(t):
+        tile_copy(t)[3].wait()
 
 
 def body(
@@ -105,25 +125,27 @@
     def arrived(dst, sem):
         pltpu.make_async_copy(dst, dst, sem).wait()
 
+    mid = here // 2
     line = jnp.broadcast_to(table[ROWS + 1 : ROWS + 2, :], (here, here))
-    toeplitz = pltpu.roll(line, 0, 1, stride=1, stride_axis=0).T
-    target = lax.broadcasted_iota(jnp.int32, (here, here), 0)
-    source = lax.broadcasted_iota(jnp.int32, (here, here), 1)
-    lag = target - source
-    own = lag >= 0
-    lag = jnp.where(own, lag, lag + here)
-    arc_here = jnp.broadcast_to(table[pl.ds(row, 1), :], (here, here))
-    arc_before = jnp.broadcast_to(table[pl.ds(jnp.maximum(row - 1, 0), 1), :], (here, here))
-    arc_before = jnp.where(row > 0, arc_before, -1.0)
-    arc_target = arc_here.T
-    arc_source = jnp.where(own, arc_here, arc_before)
-    limit = jnp.zeros((here, here), jnp.float32)
+    shifted = pltpu.roll(line, 0, 1, stride=1, stride_axis=0)
+    arc_here = table[pl.ds(row, 1), :]
+    arc_before = jnp.where(row > 0, table[pl.ds(jnp.maximum(row - 1, 0), 1), :], -1.0)
+    counts = jnp.zeros((1, here), jnp.float32)
     for a in range(arcs):
-        count = jnp.broadcast_to(table[ROWS + 2 : ROWS + 3, a : a + 1], (here, here))
-        limit = jnp.where(arc_target == a, count, limit)
-    rows_f = jnp.where(
-        (arc_target == arc_source) & (lag.astype(jnp.float32) < limit) & (lag < taps), toeplitz, 0.0
-    )
+        counts = jnp.where(arc_here == a, table[ROWS + 2 : ROWS + 3, a : a + 1], counts)
+
+    def filter_rows(start):
+        shape = (mid, here)
+        lag = lax.broadcasted_iota(jnp.int32, shape, 0) + start - lax.broadcasted_iota(jnp.int32, shape, 1)
+        own = lag >= 0
+        lag = jnp.where(own, lag, lag + here)
+        arc_target = jnp.broadcast_to(arc_here[:, start : start + mid], (mid, mid)).T
+        limit = jnp.broadcast_to(counts[:, start : start + mid], (mid, mid)).T
+        arc_target = jnp.concatenate([arc_target, arc_target], axis=1)
+        limit = jnp.concatenate([limit, limit], axis=1)
+        arc_source = jnp.where(own, arc_here, arc_before)
+        used = (arc_target == arc_source) & (lag.astype(jnp.float32) < limit) & (lag < taps)
+        return own, jnp.where(used, shifted[:, start : start + mid].T, 0.0)
 
     def three(value):
         high = value.astype(jnp.bfloat16)
@@ -131,7 +153,6 @@
         middle = rest.astype(jnp.bfloat16)
         return high, middle, (rest - middle.astype(jnp.float32)).astype(jnp.bfloat16)
 
-    mid = here // 2
     by_lane = (((1,), (1,)), ((), ()))
 
     def total(terms, value):
@@ -147,12 +168,9 @@
     def lanes_of(r, h):
         return pl.ds(pl.multiple_of(h * half + r * mid, mid), mid)
 
-    late = three(rows_f[mid:, :])
+    late = three(filter_rows(mid)[1])
     cols[0:width, lanes_of(row, H)] = total(late, design_ref[...]).T.astype(jnp.bfloat16)
     cols[width : width + EXTRA, lanes_of(row, H)] = total_lanes(late, obs_own[...]).astype(jnp.bfloat16)
-    early = three(jnp.where(own, rows_f, 0.0)[0:mid, 0:mid])
-    before = three(jnp.where(own, 0.0, rows_f)[0:mid, here - 2 * taps :])
-
     def shard(r, h):
         return cols.at[:, lanes_of(r, h)]
 
@@ -165,7 +183,7 @@
     near_first = [1, 7, 2, 6, 3, 5, 4]
 
     def pass_parts(h):
-        for i in near_first:
+        for i in near_first[::-1]:
             q = lax.rem(z + i, NZ)
             send(own_part(q, h), parts.at[h, z], part_send.at[h, i], part_recv.at[h, i], {"z": q})
 
@@ -324,6 +342,9 @@
     col_y(H)
     col_x(H)
 
+    own, rows_f = filter_rows(0)
+    early = three(jnp.where(own, rows_f, 0.0)[:, 0:mid])
+    before = three(jnp.where(own, 0.0, rows_f)[:, here - 2 * taps :])
     arrived(halo.at[taps : 2 * taps, :], halo_recv.at[0])
     arrived(halo_obs, halo_recv.at[1])
     white = total(early, design_ref[0:mid, :]) + total(before, halo[...])
@@ -388,10 +409,10 @@
     lo_arrived(3)
     lo_arrived(5)
     group(3)
+    group(5)
     arrived(early_rows(far, 0), z_recv.at[UP, 4, EARLY_OWN])
     onward(far, 4, EARLY_OWN)
     arrived(early_rows(far, 1), z_recv.at[DOWN, 4, EARLY_OTHER])
-    group(5)
     lo_arrived(4)
     group(4)
 
@@ -449,7 +470,7 @@
         ),
         in_specs=[vmem, vmem, vmem],
         out_specs=(pl.BlockSpec(memory_space=pl.ANY), vmem),
-        scratch_shapes=[pltpu.VMEM((4, len(LATER), part, width), f32), dma((NZ,))],
+        scratch_shapes=[pltpu.VMEM((4, len(LATER), part, width), f32), dma((NZ,)), dma((3 * len(LATER),))],
         compiler_params=pltpu.CompilerParams(vmem_limit_bytes=LIMIT2 * 1024 * 1024),
     )(done, cols, panel)
     return normal.reshape(4 * width, width), right

time: 84.6 us -> 83.3 us (0.985)
  Pallas kernels: 82.1 us -> 80.8 us
    pallas_call x1, Pallas kernels: 5.35 us -> 4.29 us  [on_device(): pl.pallas_call(finish, out_shape=(jax.ShapeDtypeStruct((4, NZ, part, widt...]
where the time goes in v4:
time: 83.3 us; the launch traced here: 83.2 us
  Pallas kernels  80.8 us (97%)
  local copies, waits for them, and re-layouts  0.99 us (1%)
    pallas_call x1, Pallas kernels, on_device(): pl.pallas_call(functools.partial(body, taps, arcs), out_shape=(jax.ShapeD...  76.5 us
    pallas_call x1, Pallas kernels, on_device(): pl.pallas_call(finish, out_shape=(jax.ShapeDtypeStruct((4, NZ, part, widt...  4.29 us

profile of v4, /device:TPU:1, one launch (start us, length us, event | category | flops | bytes accessed | tf_op | source)
XLA Modules:
  0.0 83.2 jit_solution(5005174039699086942)
XLA Ops:
  0.6 0.7 convert_add_fusion.table_ref
  1.4 0.0 copy-start
  1.4 1.0 %copy-done = bf16[256,768]{1,0:T(8,128)(2,1)S(1)} copy-done((bf16[256,768]{1,0:T(8,128)(2,1)S(1)}, bf16[256,768]{1,0:T(8,128)(2,1)}, u32[]{:S(2)}) %copy-start) | copy-done | bytes 393240
  2.4 76.5 %shard_map.68 = (f32[4,8,96,768]{3,2,1,0:T(8,128)S(1)}, bf16[784,2048]{1,0:T(8,128)(2,1)S(1)}, bf16[8,4,96,2048]{3,2,1,0:T(8,128)(2,1)S(1)}) custom-call(bf16[256,768]{1,0:T(8,128)(2,1)S(1)} %copy-done, f32[4096]{0:T(1024)S(1)} %convert_add_fusion.table_ref), custom_call_target="tpu_custom_call" | custom-call | tf_op jit(solution)/shard_map/pallas_call | solution.py:442
  78.9 4.3 %shard_map.69 = (f32[4,8,96,768]{3,2,1,0:T(8,128)}, f32[768]{0:T(1024)}) custom-call(f32[4,8,96,768]{3,2,1,0:T(8,128)S(1)} %get-tuple-element.7.done, bf16[784,2048]{1,0:T(8,128)(2,1)S(1)} %get-tuple-element.8.cols, bf16[8,4,96,2048]{3,2,1,0:T(8,128)(2,1)S(1)} %get-tuple-element.9.panel), custom_call_target="tpu_custom_call" | custom-call | tf_op jit(solution)/shard_map/pallas_call | solution.py:465
Async XLA Ops:
  1.4 1.0 %copy-start = (bf16[256,768]{1,0:T(8,128)(2,1)S(1)}, bf16[256,768]{1,0:T(8,128)(2,1)}, u32[]{:S(2)}) copy-start(bf16[256,768]{1,0:T(8,128)(2,1)} %design_ref.1) | copy-start | bytes 1179652

commit v5 on v4

--- a/solution.py
+++ b/solution.py
@@ -398,6 +398,7 @@
     hop(3, EARLY_OTHER)
     lo_arrived(6)
     group(2)
+    group(6)
     far = lax.rem(z + 4, NZ)
     for way in (UP, DOWN):
         arrived(halves(far, way), z_recv.at[way, 4, HALF])
@@ -405,7 +406,6 @@
     for way in LATE_SIDES:
         arrived(late_side(far, way), z_recv.at[way, 4, LATE])
     onward(far, 4, LATE)
-    group(6)
     lo_arrived(3)
     lo_arrived(5)
     group(3)

time: 83.3 us -> 85 us (1.020)
  Pallas kernels: 80.8 us -> 82.4 us
    pallas_call x1, Pallas kernels: 76.5 us -> 78.1 us  [on_device(): pl.pallas_call(functools.partial(body, taps, arcs), out_shape=(jax.ShapeD...]
where the time goes in v5:
time: 85 us; the launch traced here: 84.8 us
  Pallas kernels  82.4 us (97%)
  local copies, waits for them, and re-layouts  0.99 us (1%)
    pallas_call x1, Pallas kernels, on_device(): pl.pallas_call(functools.partial(body, taps, arcs), out_shape=(jax.ShapeD...  78.1 us
    pallas_call x1, Pallas kernels, on_device(): pl.pallas_call(finish, out_shape=(jax.ShapeDtypeStruct((4, NZ, part, widt...  4.29 us

profile of v5, /device:TPU:1, one launch (start us, length us, event | category | flops | bytes accessed | tf_op | source)
XLA Modules:
  0.0 84.8 jit_solution(3580900551291536847)
XLA Ops:
  0.6 0.7 convert_add_fusion.table_ref
  1.4 0.0 copy-start
  1.4 1.0 %copy-done = bf16[256,768]{1,0:T(8,128)(2,1)S(1)} copy-done((bf16[256,768]{1,0:T(8,128)(2,1)S(1)}, bf16[256,768]{1,0:T(8,128)(2,1)}, u32[]{:S(2)}) %copy-start) | copy-done | bytes 393240
  2.4 78.1 %shard_map.68 = (f32[4,8,96,768]{3,2,1,0:T(8,128)S(1)}, bf16[784,2048]{1,0:T(8,128)(2,1)S(1)}, bf16[8,4,96,2048]{3,2,1,0:T(8,128)(2,1)S(1)}) custom-call(bf16[256,768]{1,0:T(8,128)(2,1)S(1)} %copy-done, f32[4096]{0:T(1024)S(1)} %convert_add_fusion.table_ref), custom_call_target="tpu_custom_call" | custom-call | tf_op jit(solution)/shard_map/pallas_call | solution.py:442
  80.5 4.3 %shard_map.69 = (f32[4,8,96,768]{3,2,1,0:T(8,128)}, f32[768]{0:T(1024)}) custom-call(f32[4,8,96,768]{3,2,1,0:T(8,128)S(1)} %get-tuple-element.7.done, bf16[784,2048]{1,0:T(8,128)(2,1)S(1)} %get-tuple-element.8.cols, bf16[8,4,96,2048]{3,2,1,0:T(8,128)(2,1)S(1)} %get-tuple-element.9.panel), custom_call_target="tpu_custom_call" | custom-call | tf_op jit(solution)/shard_map/pallas_call | solution.py:465
Async XLA Ops:
  1.4 1.0 %copy-start = (bf16[256,768]{1,0:T(8,128)(2,1)S(1)}, bf16[256,768]{1,0:T(8,128)(2,1)}, u32[]{:S(2)}) copy-start(bf16[256,768]{1,0:T(8,128)(2,1)} %design_ref.1) | copy-start | bytes 1179652
